TPU v7x, 512 devices: a whole 4x4x16 slice. The times are simulated.
512 devices in a mesh: ctx: 32 (over y, x, core), exp: 16 (over z).
Axes of the slice: x: 4, y: 4, z: 16, core: 2. Of those that a mesh axis runs over, the one named last changes fastest.
Arguments:
- queries: bfloat16 [8192, 4096], P('ctx', 'exp'), may hold values from -6 to 6
- key_rows: bfloat16 [8192, 4096], P('ctx', 'exp'), may hold values from -6 to 6
- value_rows: bfloat16 [8192, 4096], P('ctx', 'exp'), may hold values from -6 to 6
- decay_rate: float32 [32], P('exp'), may hold values from 4.8828124e-06 to 0.06
- out_weight: bfloat16 [4096, 3072], P('exp', 'ctx'), may hold values from -0.09375 to 0.09375
- residual: bfloat16 [8192, 3072], P(('ctx', 'exp')), may hold values from -6 to 6
- moe_gain: float32 [3072], replicated, may hold values from 0.1 to 1.9
- expert_ids: int32 [8192, 2], P(('ctx', 'exp')), may hold values from 0 to 15, all different within a row; in each aligned block of 16 rows (0 to 15, 16 to 31, ...) at most 3 rows name the same one
- gate_weight: bfloat16 [16, 4608, 3072], P('exp', 'ctx'), may hold values from -0.109375 to 0.109375
- up_weight: bfloat16 [16, 4608, 3072], P('exp', 'ctx'), may hold values from -0.109375 to 0.109375
Outputs:
- mixed: bfloat16 [8192, 3072], P(('ctx', 'exp'))
- expert_hidden: bfloat16 [16, 4608, 1536], P('exp', 'ctx')
Inputs may be any that keep to these rules, and one draw needn't show every extreme that they name: `expert_ids`: in each aligned block of 16 tokens (the rows of one device) no expert is named by more than 3 of the block's routes; some block names some expert exactly 3 times; a token's two ids differ.
All inputs are finite; a program needn't handle non-finite values.
Results may differ from a plain program's by a relative error of at most 0.0079.
Values may be sent and summed in bfloat16 or wider, within the bound.
A program may use at most 64 MiB of HBM per device.

v0:
```python
import jax
import jax.numpy as jnp
from jax import lax
from jax.sharding import PartitionSpec as P


def entering(value, axis, combine, identity):
    devices, position = (lax.axis_size(axis), lax.axis_index(axis))
    everything = jax.tree.map(lambda part: lax.all_gather(part, axis), value)
    start = jax.tree.map(
        lambda part, zero: jnp.broadcast_to(jnp.asarray(zero, part.dtype), part.shape),
        value,
        identity,
    )

    def hop(k, before):
        reached = k < position
        new = combine(before, jax.tree.map(lambda part: part[k], everything))
        return jax.tree.map(lambda a, b: jnp.where(reached, a, b), new, before)

    return lax.fori_loop(0, devices, hop, start)


def route_slots(id_rows):
    count = id_rows.shape[1]
    same = id_rows[:, :, None] == id_rows[:, None, :]
    before = lax.broadcasted_iota(jnp.int32, (count, count), 1) < lax.broadcasted_iota(
        jnp.int32, (count, count), 0
    )
    return jnp.sum((same & before[None]).astype(jnp.int32), axis=2)


def select_matrix(id_rows, slot_rows, owners, capacity):
    routes = id_rows.shape[1]
    places = jnp.arange(capacity, dtype=jnp.int32)
    hits = (id_rows[:, None, None, :] == owners[None, :, None, None]) & (
        slot_rows[:, None, None, :] == places[None, None, :, None]
    )
    to_token = (
        jnp.arange(routes, dtype=jnp.int32)[:, None] // 2
        == jnp.arange(routes // 2, dtype=jnp.int32)[None, :]
    ).astype(jnp.float32)
    return jnp.einsum("bepr,rt->bept", hits.astype(jnp.float32), to_token)


def per_device(
    queries,
    key_rows,
    value_rows,
    decay_rate,
    out_weight,
    residual,
    moe_gain,
    expert_ids,
    gate_weight,
    up_weight,
):
    highest = lax.Precision.HIGHEST
    block_len = queries.shape[0]
    heads_here = decay_rate.shape[0]
    width_here = queries.shape[1]
    head_size = width_here // heads_here
    model_width = residual.shape[1]
    exp_count = lax.axis_size("exp")
    tok_count = block_len // exp_count
    capacity = max(2, 3 * tok_count // exp_count)
    query_here = queries.reshape(block_len, heads_here, head_size)
    key_here = key_rows.reshape(block_len, heads_here, head_size)
    value_here = value_rows.reshape(block_len, heads_here, head_size)
    position = jnp.arange(block_len, dtype=jnp.float32)
    offset = position[:, None] - position[None, :]
    masked = jnp.where(
        (offset >= 0)[None],
        jnp.exp(-decay_rate[:, None, None] * jnp.maximum(offset, 0.0)[None]),
        0.0,
    )
    inner = jnp.exp(-decay_rate[None, :] * position[:, None])
    tail = jnp.exp(-decay_rate[None, :] * (block_len - position[:, None]))
    whole = jnp.exp(-decay_rate * block_len)
    scores = jnp.einsum("ihd,jhd->hij", query_here, key_here, preferred_element_type=jnp.float32)
    weighted = (scores * masked).astype(jnp.bfloat16)
    local_part = jnp.einsum(
        "hij,jhd->ihd", weighted, value_here, preferred_element_type=jnp.float32
    )
    fresh = jnp.einsum(
        "jhd,jhe->hde",
        key_here.astype(jnp.float32) * tail[:, :, None],
        value_here.astype(jnp.float32),
        precision=highest,
    )

    def combine(earlier, later):
        return (earlier[0] * later[0], later[0][:, None, None] * earlier[1] + later[1])

    unused, state_in = entering(
        (whole, fresh), "ctx", combine, (jnp.ones_like(whole), jnp.zeros_like(fresh))
    )
    carried = (
        jnp.einsum("ihd,hde->ihe", query_here.astype(jnp.float32), state_in, precision=highest)
        * inner[:, :, None]
    )
    attended = local_part + carried
    scale_rows = lax.rsqrt(jnp.mean(attended * attended, axis=-1, keepdims=True) + 1e-05)
    head_out = (attended * scale_rows).astype(jnp.bfloat16).reshape(block_len, width_here)
    partial_rows = jnp.dot(
        head_out,
        lax.all_gather(out_weight, "ctx", axis=1, tiled=True),
        preferred_element_type=jnp.float32,
    )
    attn = lax.psum_scatter(partial_rows, "exp", scatter_dimension=0, tiled=True)
    mixed = (residual.astype(jnp.float32) + attn).astype(jnp.bfloat16)
    mixed_f = mixed.astype(jnp.float32)
    normed = (
        mixed_f * lax.rsqrt(jnp.mean(mixed_f * mixed_f, axis=-1, keepdims=True) + 1e-05) * moe_gain
    ).astype(jnp.bfloat16)
    peer_rows, peer_ids = (
        lax.all_gather(normed, "exp", axis=0, tiled=True),
        lax.all_gather(expert_ids.astype(jnp.bfloat16), "exp", axis=0, tiled=True),
    )
    id_rows = peer_ids.astype(jnp.int32).reshape(exp_count, 2 * tok_count)
    slot_rows = route_slots(id_rows)
    owner = jnp.reshape(lax.axis_index("exp"), (1,))
    picks = select_matrix(id_rows, slot_rows, owner, capacity)[:, 0].astype(jnp.bfloat16)
    chosen = jnp.einsum(
        "bpt,btd->bpd",
        picks,
        peer_rows.reshape(exp_count, tok_count, model_width),
        preferred_element_type=jnp.float32,
    )
    received = chosen.astype(jnp.bfloat16).reshape(exp_count * capacity, model_width)
    gate_here = gate_weight[0]
    up_here = up_weight[0]
    contract = (((1,), (1,)), ((), ()))
    piece = lax.all_gather(received, "ctx", axis=0, tiled=True)
    gated = lax.dot_general(gate_here, piece, contract, preferred_element_type=jnp.float32)
    lifted = lax.dot_general(up_here, piece, contract, preferred_element_type=jnp.float32)
    hidden = (jax.nn.silu(gated) * lifted).astype(jnp.bfloat16)
    return (mixed, hidden[None])


def solution(mesh):
    in_specs = (
        P("ctx", "exp"),
        P("ctx", "exp"),
        P("ctx", "exp"),
        P("exp"),
        P("exp", "ctx"),
        P(("ctx", "exp"), None),
        P(),
        P(("ctx", "exp"), None),
        P("exp", "ctx", None),
        P("exp", "ctx", None),
    )
    out_specs = (P(("ctx", "exp"), None), P("exp", "ctx", None))
    return jax.shard_map(
        per_device, mesh=mesh, in_specs=in_specs, out_specs=out_specs, check_vma=False
    )
```

profile of v0, /device:TPU:1, one launch (start us, length us, event | category | flops | bytes accessed | tf_op | source)
XLA Modules:
  0.0 382.5 jit_solution(13646248206387030863)
XLA Ops:
  7.3 1.1 copy.64
  8.4 1.3 dynamic-slice
  11.1 1.8 fusion.14
  13.9 69.0 %all-reduce = f32[64]{0:T(128)S(1)} all-reduce(f32[64]{0:T(128)S(1)} %get-tuple-element.130), channel_id=2, replica_groups=mesh['ctx'=32,'exp'=16] {'ctx'}, use_global_device_ids=true, to_apply=%add | all-reduce | flops 64 | bytes 512
  83.1 33.2 %while.14 = (s32[]{:T(128)}, f32[2,128,128]{2,1,0:T(8,128)S(1)}, s32[]{:T(128)}, f32[32,2]{1,0:T(8,128)S(1)}, f32[32,2,128,128]{3,2,1,0:T(8,128)}, /*index=5*/s32[]{:T(128)}, s32[]{:T(128)}) while((s32[]{:T(128)}, f32[2,128,128]{2,1,0:T(8,128)S(1)}, s32[]{:T(128)}, f32[32,2]{1,0:T(8,128)S(1)}, f32[32,2,128,128]{3,2,1,0:T(8,128)}, ...), condition=%wide.region_1.2_spmd.clone, body=%wide.region_0.1_spmd.clone.sunk | while | flops 131076 | bytes 393353 | solution.py:21
  85.2 1.0 fusion.62
  88.3 1.0 fusion.62
  89.3 1.0 fusion.62
  92.4 1.0 fusion.62
  93.5 1.0 fusion.62
  98.7 1.0 fusion.62
  99.7 1.0 fusion.62
  105.9 1.0 fusion.62
  108.0 1.0 fusion.62
  117.1 24.0 %all-gather.8.cloned.1.call-done = bf16[256,3072]{0,1:T(8,128)(2,1)} async-done(((bf16[256,96]{0,1:T(8,128)(2,1)}), bf16[256,3072]{0,1:T(8,128)(2,1)}) %all-gather.8.cloned.1.call-update) | async-done | bytes 1572880 | tf_op jit(solution)/shard_map/all_gather | solution.py:107
  141.1 3.7 fusion.49
  144.8 67.0 %reduce-scatter.2.cloned.1.call-done = f32[16,3072]{1,0:T(8,128)} async-done(((f32[256,3072]{1,0:T(8,128)}), f32[16,3072]{1,0:T(8,128)}) %reduce-scatter.2.cloned.1.call-update) | async-done | bytes 196624 | tf_op jit(solution)/shard_map/reduce_scatter | solution.py:110
  211.8 1.1 fusion.23
  213.7 20.9 %all-gather.2 = bf16[16,16,2]{1,2,0:T(2,128)(2,1)S(1)} all-gather(bf16[1,16,2]{1,2,0:T(2,128)(2,1)S(1)} %convert_bitcast_fusion), channel_id=1, replica_groups=mesh['ctx'=32,'exp'=16] {'exp'}, dimensions={0}, use_global_device_ids=true | all-gather | bytes 1088 | tf_op jit(solution)/shard_map/all_gather | solution.py:118
  235.5 47.9 %all-gather.10.cloned.1.call-done = bf16[256,3072]{1,0:T(8,128)(2,1)} async-done(((bf16[16,3072]{1,0:T(8,128)(2,1)}), bf16[256,3072]{1,0:T(8,128)(2,1)}) %all-gather.10.cloned.1.call-update) | async-done | bytes 1572880 | tf_op jit(solution)/shard_map/all_gather | solution.py:117
  283.4 1.8 convolution_convert_fusion
  286.2 78.5 %all-gather.12.cloned.1.call-done = bf16[1536,3072]{1,0:T(8,128)(2,1)} async-done(((bf16[48,3072]{1,0:T(8,128)(2,1)}), bf16[1536,3072]{1,0:T(8,128)(2,1)}) %all-gather.12.cloned.1.call-update) | async-done | bytes 9437200 | tf_op jit(solution)/shard_map/all_gather | solution.py:134
  364.8 7.1 %convolution_bitcast_fusion.1 = f32[144,1536]{1,0:T(8,128)S(1)} fusion(bf16[1536,3072]{1,0:T(8,128)(2,1)} %all-gather.12.cloned.1.call-done, bf16[1,144,3072]{2,1,0:T(8,128)(2,1)S(1)} %copy-done), kind=kOutput, calls=%fused_computation.6 | convolution fusion | flops 1358954496 | bytes 11206656 | tf_op jit(solution)/shard_map/dot_general | solution.py:135
  371.9 4.1 %fusion.3 = bf16[1,144,1536]{2,1,0:T(8,128)(2,1)} fusion(bf16[1536,3072]{1,0:T(8,128)(2,1)S(1)} %copy-done.6, bf16[1,144,3072]{2,1,0:T(8,128)(2,1)S(1)} %copy-done.7, f32[144,1536]{1,0:T(8,128)S(1)} %convolution_bitcast_fusion.1), kind=kOutput, calls=%fused_computation.8 | convolution fusion | flops 1360281600 | bytes 11649024 | tf_op jit(solution)/shard_map/dot_general | solution.py:136
  (109 shorter events, 28.6 us)
Async XLA Ops:
  7.2 357.6 %copy-start = (bf16[1,144,3072]{2,1,0:T(8,128)(2,1)S(1)}, bf16[1,144,3072]{2,1,0:T(8,128)(2,1)}, u32[]{:S(2)}) copy-start(bf16[1,144,3072]{2,1,0:T(8,128)(2,1)} %param.20) | copy-start | bytes 2654212
  7.2 109.4 %copy-start.2 = (bf16[256,256]{1,0:T(8,128)(2,1)S(1)}, bf16[256,256]{1,0:T(8,128)(2,1)}, u32[]{:S(2)}) copy-start(bf16[256,256]{1,0:T(8,128)(2,1)} %param.14) | copy-start | bytes 393220
  7.2 109.1 %copy-start.3 = (bf16[256,256]{1,0:T(8,128)(2,1)S(1)}, bf16[256,256]{1,0:T(8,128)(2,1)}, u32[]{:S(2)}) copy-start(bf16[256,256]{1,0:T(8,128)(2,1)} %param.12) | copy-start | bytes 393220
  7.2 75.8 %all-gather.14.cloned.1.call-start = ((), (), s32[]{:S(2)}) async-start(), calls=%async_computation.5 | async-start | bytes 4325376 | tf_op jit(solution)/shard_map/all_gather | solution.py:9
  13.0 128.1 %all-gather.8.cloned.1.call-start = ((), (), s32[]{:S(2)}) async-start(), calls=%async_computation.1 | async-start | bytes 1622016 | tf_op jit(solution)/shard_map/all_gather | solution.py:107
  13.7 198.1 %reduce-scatter.2.cloned.1.call-start = ((), (), s32[]{:S(2)}) async-start(), calls=%async_computation.2 | async-start | bytes 3342336 | tf_op jit(solution)/shard_map/reduce_scatter | solution.py:110
  141.0 70.8 %copy-start.4 = (bf16[16,3072]{1,0:T(8,128)(2,1)S(1)}, bf16[16,3072]{1,0:T(8,128)(2,1)}, u32[]{:S(2)}) copy-start(bf16[16,3072]{1,0:T(8,128)(2,1)} %param.17) | copy-start | bytes 294916
  141.0 71.9 %copy-start.5 = (f32[3072]{0:T(1024)S(1)}, f32[3072]{0:T(1024)}, u32[]{:S(2)}) copy-start(f32[3072]{0:T(1024)} %param.18) | copy-start | bytes 36868
  141.0 72.7 %copy-start.8 = (s32[16,2]{0,1:T(2,128)S(1)}, s32[16,2]{0,1:T(2,128)}, u32[]{:S(2)}) copy-start(s32[16,2]{0,1:T(2,128)} %param.19) | copy-start | bytes 388
  144.8 138.7 %all-gather.10.cloned.1.call-start = ((), (), s32[]{:S(2)}) async-start(), calls=%async_computation.3 | async-start | bytes 1671168 | tf_op jit(solution)/shard_map/all_gather | solution.py:117
  212.9 159.0 %copy-start.1 = (bf16[16,3072]{1,0:T(8,128)(2,1)}, bf16[16,3072]{1,0:T(8,128)(2,1)S(1)}, u32[]{:S(2)}) copy-start(bf16[16,3072]{1,0:T(8,128)(2,1)S(1)} %get-tuple-element.126) | copy-start | bytes 294916
  213.7 151.1 %all-gather.12.cloned.1.call-start = ((), (), s32[]{:S(2)}) async-start(), calls=%async_computation.4 | async-start | bytes 9732096 | tf_op jit(solution)/shard_map/all_gather | solution.py:134
  286.2 85.7 %copy-start.7 = (bf16[1,144,3072]{2,1,0:T(8,128)(2,1)S(1)}, bf16[1,144,3072]{2,1,0:T(8,128)(2,1)}, u32[]{:S(2)}) copy-start(bf16[1,144,3072]{2,1,0:T(8,128)(2,1)} %param.21) | copy-start | bytes 2654212
  364.8 7.1 %copy-start.6 = (bf16[1536,3072]{1,0:T(8,128)(2,1)S(1)}, bf16[1536,3072]{1,0:T(8,128)(2,1)}, u32[]{:S(2)}) copy-start(bf16[1536,3072]{1,0:T(8,128)(2,1)} %all-gather.12.cloned.1.call-done) | copy-start | bytes 28311556
Sparse Core Ops, SparseCore 0:
  13.1 67.0 all-gather.13
  83.3 57.7 all-gather.7
  144.9 66.8 reduce-scatter.1
  214.3 69.0 all-gather.9
  287.0 77.7 all-gather.11
where the time goes:
time: 383 us; the launch traced here: 382 us
  waiting for transfers between devices  218 us (57%)
  blocking collectives  89.9 us (23%)
  other arithmetic  35.2 us (9%)
  matrix products  19.3 us (5%)
  between operations  14.7 us (4%)
  local copies, waits for them, and re-layouts  3.99 us (1%)
    all_gather x1, waiting for transfers between devices, per_device(): piece = lax.all_gather(received, 'ctx', axis=0, tiled=True)  78.5 us
    unnamed x1, blocking collectives  69 us
    reduce_scatter x1, waiting for transfers between devices, per_device(): lax.psum_scatter(partial_rows, 'exp', scatter_dimension=0, tiled=True)  67 us
    all_gather x1, waiting for transfers between devices, per_device(): lax.all_gather(normed, 'exp', axis=0, tiled=True)  47.9 us
    select_n x32, other arithmetic, hop(): return jax.tree.map(lambda a, b: jnp.where(reached, a, b), new, before)  31.9 us
    all_gather x1, waiting for transfers between devices, per_device(): lax.all_gather(out_weight, 'ctx', axis=1, tiled=True)  24 us
    all_gather x1, blocking collectives, per_device(): lax.all_gather(expert_ids.astype(jnp.bfloat16), 'exp', axis=0, tiled=True)  20.9 us
  transfers between devices with their start and end apart: 5, of which 4 were waited for; matrix products, arithmetic and copies ran while one was open for 9% of the time, Pallas kernels for 0%

commit v1 on v0

v1 whole, which is shorter than its diff:
```python
import jax
import jax.numpy as jnp
from jax import lax
from jax.experimental import pallas as pl
from jax.experimental.pallas import tpu as pltpu
from jax.sharding import PartitionSpec as P

MESH = pl.DeviceIdType.MESH
F32 = jnp.float32
BF16 = jnp.bfloat16

SIDE = 4
NZ = 16
SPAN = 256
HD = 128
WIDTH = 3072
OWN_COLS = 96
TOK = 16
CAP = 3
ROWS = NZ * CAP
CHUNKS = 3
CW = WIDTH // CHUNKS
KB = CW // 128
PIECES = 6
PW = WIDTH // PIECES
HID_HERE = 144
SLOTS = 1536

A1, A2, B1A, B1B, B2A, B2B, XC, SENT = range(8)


def nt(a, b):
    return lax.dot_general(a, b, (((1,), (1,)), ((), ())), preferred_element_type=F32)


def nn(a, b):
    return jnp.dot(a, b, preferred_element_type=F32)


def iota(shape, dim):
    return lax.broadcasted_iota(jnp.int32, shape, dim)


def one_hot(test):
    return jnp.where(test, 1.0, 0.0).astype(BF16)


def split(x):
    hi = x.astype(BF16)
    return hi, (x - hi.astype(F32)).astype(BF16)


class Gather:
    def __init__(self, whole, half, span, sems, z, core, a, b):
        self.whole, self.half, self.span, self.sems = whole, half, span, sems
        self.z, self.core, self.a, self.b = z, core, a, b

    def at(self, da, db):
        a, b = lax.rem(self.a + (da + SIDE), SIDE), lax.rem(self.b + (db + SIDE), SIDE)
        return self.core + a * (2 + 6 * self.core) + b * (8 - 6 * self.core)

    def send(self, ref, sem, ctx):
        pltpu.make_async_remote_copy(
            src_ref=ref,
            dst_ref=ref,
            send_sem=self.sems.at[SENT],
            recv_sem=self.sems.at[sem],
            device_id=(ctx, self.z),
            device_id_type=MESH,
        ).start()

    def wait(self, sem, blocks):
        ref = self.span(blocks)
        pltpu.make_async_copy(ref, ref, self.sems.at[sem]).wait()

    def across(self, block):
        self.send(self.whole(block), XC, self.at(0, 0) + 1 - 2 * self.core)

    def start(self):
        own = self.whole(self.at(0, 0))
        for d in (1, -1):
            self.send(own, A1, self.at(d, 0))
        for d in (1, -1):
            self.send(own, B1A, self.at(0, d))
        self.across(self.at(0, 0))

    def step1(self):
        self.wait(A1, 2)
        for d in (1, -1):
            block = self.at(-d, 0)
            self.send(self.half(block, (1 - d) // 2), A2, self.at(d, 0))
        for d in (1, -1):
            block = self.at(-d, 0)
            for e in (1, -1):
                self.send(self.whole(block), B1A, self.at(0, e))
            self.across(block)

    def step2(self):
        self.wait(A2, 1)
        block = self.at(2, 0)
        for e in (1, -1):
            self.send(self.whole(block), B1B, self.at(0, e))
        self.across(block)

    def relay(self, da, sem):
        for e in (1, -1):
            block = self.at(da, -e)
            self.send(self.half(block, (1 - e) // 2), sem, self.at(0, e))
            self.across(block)

    def step3(self):
        self.wait(B1A, 6)
        for da in (0, 1, -1):
            self.relay(da, B2A)

    def step4(self):
        self.wait(B1B, 2)
        self.relay(2, B2B)

    def step5(self):
        self.wait(B2A, 3)
        for da in (0, 1, -1):
            self.across(self.at(da, 2))
        self.wait(B2B, 1)
        self.across(self.at(2, 2))

    def arrived(self):
        self.wait(XC, 16)

    def finish(self):
        self.wait(SENT, 31)


def kernel(
    decay, q_hbm, k_hbm, v_hbm, w_hbm, res_hbm, gain_hbm, ids_hbm, gate_hbm, up_hbm,
    mixed_out, hidden_out,
    qb, kb, vb, wb, resb, gainb, idsb, wg, full_w, fr, e1, fx, fy, st, sto, att, ho,
    part, sb, rb, mixf, pick, perm, msg, got, slots, acc,
    load_sem, st_sem, gw_sem, gs_sem, rs_recv, rs_send, c_recv, c_send,
):
    me, z = lax.axis_index("ctx"), lax.axis_index("exp")
    core = lax.rem(me, 2)
    x = lax.rem(me // 2, SIDE)
    y = me // (2 * SIDE)
    a, b = x + core * (y - x), y + core * (x - y)
    partner = me + 1 - 2 * core

    def x_peer(d):
        return me + (lax.rem(x + d, SIDE) - x) * 2

    def y_peer(d):
        return me + (lax.rem(y + d, SIDE) - y) * (2 * SIDE)

    def z_peer(d):
        return lax.rem(z + d, NZ)

    barrier = pltpu.get_barrier_semaphore()

    def greet(ctx, exp):
        pl.semaphore_signal(barrier, inc=1, device_id=(ctx, exp), device_id_type=MESH)

    greet(partner, z)
    for d in range(1, SIDE):
        greet(x_peer(d), z)
        greet(y_peer(d), z)

    @pl.loop(1, NZ)
    def _(d):
        greet(me, z_peer(d))

    loads = [
        pltpu.make_async_copy(src, dst, load_sem.at[i])
        for i, (src, dst) in enumerate(
            (
                (k_hbm, kb), (v_hbm, vb), (w_hbm, wb), (q_hbm, qb), (ids_hbm, idsb),
                (res_hbm, resb), (gain_hbm, gainb),
                (gate_hbm.at[0], full_w.at[pl.ds(0, HID_HERE)]),
                (up_hbm.at[0], full_w.at[pl.ds(HID_HERE, HID_HERE)]),
            )
        )
    ]
    for load in loads:
        load.start()

    eye = one_hot(iota((HD, HD), 0) == iota((HD, HD), 1))

    loads[0].wait()
    loads[1].wait()
    for h in range(2):
        cols = pl.ds(h * HD, HD)
        rate = decay[h]
        tail = jnp.exp(-rate * (SPAN - iota((1, SPAN), 1)).astype(F32))
        hi, lo = split(nt(eye, kb[:, cols]) * tail)
        value = vb[:, cols]
        fr[h] = nn(hi, value) + nn(lo, value)

    loads[2].wait()
    small = one_hot(iota((OWN_COLS, OWN_COLS), 0) == iota((OWN_COLS, OWN_COLS), 1))
    wg[me] = nt(small, wb[...]).astype(BF16)

    weights = Gather(
        lambda n: wg.at[n],
        lambda n, i: wg.at[n, :, pl.ds(i * HD, HD)],
        lambda n: wg.at[pl.ds(0, n)],
        gw_sem, z, core, a, b,
    )

    pl.semaphore_wait(barrier, 1 + 2 * (SIDE - 1) + NZ - 1)

    def state_send(src, dst, i, ctx):
        pltpu.make_async_remote_copy(
            src_ref=src,
            dst_ref=dst,
            send_sem=st_sem.at[4 + i],
            recv_sem=st_sem.at[i],
            device_id=(ctx, z),
            device_id_type=MESH,
        ).start()

    def wait_for(ref, sem):
        pltpu.make_async_copy(ref, ref, sem).wait()

    state_send(fr.at[1 - core], e1, 0, partner)
    weights.start()

    rate_core = decay[core]

    def power(blocks):
        count = jnp.full((1, HD), SPAN, jnp.int32) * blocks
        return jnp.exp(-rate_core * jnp.maximum(count, 0).astype(F32))

    def gated(test, value):
        return jnp.where(test, value, 0.0)

    def local_part(h):
        cols = pl.ds(h * HD, HD)
        rate = decay[h]
        offset = iota((SPAN, SPAN), 0) - iota((SPAN, SPAN), 1)
        masked = jnp.where(
            offset >= 0, jnp.exp(-rate * jnp.maximum(offset, 0).astype(F32)), 0.0
        )
        weighted = (nt(qb[:, cols], kb[:, cols]) * masked).astype(BF16)
        att[h] = nn(weighted, vb[:, cols])

    wait_for(e1, st_sem.at[0])
    own, other = fr[core], e1[...]
    first = jnp.where(core == 0, own, other)
    second = jnp.where(core == 0, other, own)
    e1[...] = first
    fx[x] = (power(1) * first + second).astype(BF16)
    for d in range(1, SIDE):
        state_send(fx.at[x], fx.at[x], 1, x_peer(d))

    loads[3].wait()
    local_part(0)
    weights.step1()

    wait_for(fx.at[pl.ds(0, SIDE - 1)], st_sem.at[1])
    before, total = jnp.zeros((HD, HD), F32), jnp.zeros((HD, HD), F32)
    for i in range(SIDE):
        term = fx[i].astype(F32)
        before = before + gated(i < x, power(2 * (x - 1 - i))) * term
        total = total + power(2 * (SIDE - 1 - i)) * term
    fy[y] = total.astype(BF16)
    for d in range(1, SIDE):
        state_send(fy.at[y], fy.at[y], 2, y_peer(d))

    local_part(1)
    weights.step2()
    weights.step3()

    wait_for(fy.at[pl.ds(0, SIDE - 1)], st_sem.at[2])
    above = jnp.zeros((HD, HD), F32)
    for i in range(SIDE):
        above = above + gated(i < y, power(2 * SIDE * (y - 1 - i))) * fy[i].astype(F32)
    state0 = power(2 * x) * above + before
    state1 = power(1) * state0 + e1[...]
    st[core] = jnp.where(core == 0, state0, state1)
    sto[...] = jnp.where(core == 0, state1, state0)
    state_send(sto, st.at[core], 3, partner)
    weights.step4()

    loads[4].wait()
    lane = iota((TOK, HD), 1)
    expert = lax.shift_right_logical(lane * 43, 7)
    ids = idsb[...]
    named = one_hot((ids[:, 0:1] == expert) | (ids[:, 1:2] == expert))
    lower = one_hot(iota((TOK, TOK), 0) > iota((TOK, TOK), 1))
    rank = nn(lower, named)
    place = (lane - CAP * expert).astype(F32)
    chosen = jnp.where(rank == place, named.astype(F32), 0.0).astype(BF16)
    turned = nt(eye, chosen).astype(BF16)
    tall = (ROWS * KB, HD)
    spread = one_hot(lax.shift_right_logical(iota(tall, 0), 3) == iota(tall, 1))
    again = one_hot(jnp.bitwise_and(lane, TOK - 1) == iota((TOK, HD), 0))
    table = nn(nn(spread, turned).astype(BF16), again)
    here = jnp.bitwise_and(iota(tall, 0), KB - 1) == lax.shift_right_logical(iota(tall, 1), 4)
    pick[...] = jnp.where(here, table, 0.0).astype(BF16)
    square = (ROWS * KB, ROWS * KB)
    block = lax.shift_right_logical(iota(square, 0) * 1366, 16)
    perm[...] = one_hot(iota(square, 1) == KB * (iota(square, 0) - ROWS * block) + block)

    wait_for(st.at[0], st_sem.at[3])
    weights.step5()
    for h in range(2):
        cols = pl.ds(h * HD, HD)
        query = qb[:, cols]
        hi, lo = split(st[h])
        inner = jnp.exp(-decay[h] * iota((SPAN, HD), 0).astype(F32))
        attended = att[h] + (nn(query, hi) + nn(query, lo)) * inner
        mean = jnp.mean(attended * attended, axis=-1, keepdims=True)
        ho[:, cols] = (attended * lax.rsqrt(mean + 1e-05)).astype(BF16)

    weights.arrived()

    def sign(n):
        return 1 if n < PIECES // 2 else -1

    def rs_send_to(i, n, d):
        cols = pl.ds(n * PW, PW)
        pltpu.make_async_remote_copy(
            src_ref=sb.at[i, :, cols],
            dst_ref=rb.at[i, :, cols],
            send_sem=rs_send.at[0],
            recv_sem=rs_recv.at[i, n],
            device_id=(me, z_peer(NZ + d)),
            device_id_type=MESH,
        ).start()

    def wait_piece(i, n):
        wait_for(rb.at[i, :, pl.ds(n * PW, PW)], rs_recv.at[i, n])

    SHORT = NZ // 2
    heads = ho[...]
    flat = wg[...].reshape(WIDTH, SPAN)
    for n in range(PIECES):
        cols = pl.ds(n * PW, PW)
        rows = nt(heads, flat[n * PW : (n + 1) * PW])
        part[:, :, cols] = rows.reshape(NZ, TOK, PW)
        sb[0, :, cols] = part[z_peer(8), :, cols].astype(BF16)
        rs_send_to(0, n, sign(n))
        sb[SHORT, :, cols] = part[z_peer(NZ - 7 * sign(n)), :, cols].astype(BF16)
        rs_send_to(SHORT, n, -sign(n))

    def rs_step(i, n, d, target):
        cols = pl.ds(n * PW, PW)
        wait_piece(i - 1, n)
        value = rb[i - 1, :, cols].astype(F32) + part[target, :, cols]
        sb[i, :, cols] = value.astype(BF16)
        rs_send_to(i, n, d)

    @pl.loop(1, 7)
    def _(i):
        for n in range(PIECES):
            s = sign(n)
            rs_step(i, n, s, z_peer(NZ + s * (8 - i)))
            rs_step(SHORT + i, n, -s, z_peer(NZ - s * (7 - i)))

    for n in range(PIECES):
        rs_step(7, n, sign(n), z_peer(NZ + sign(n)))

    loads[5].wait()
    loads[6].wait()
    squares = jnp.zeros((TOK, HD), F32)
    for n in range(PIECES):
        cols = pl.ds(n * PW, PW)
        wait_piece(SHORT + 6, n)
        wait_piece(7, n)
        value = part[z, :, cols] + (rb[7, :, cols].astype(F32) + rb[SHORT + 6, :, cols].astype(F32))
        rounded = (resb[:, cols].astype(F32) + value).astype(BF16)
        mixed_out[:, cols] = rounded
        rounded = rounded.astype(F32)
        mixf[:, cols] = rounded
        power2 = rounded * rounded
        for i in range(PW // HD):
            squares = squares + power2[:, i * HD : (i + 1) * HD]
    scale = lax.rsqrt(jnp.sum(squares, axis=-1, keepdims=True) / WIDTH + 1e-05)

    def c_copy(j, dest):
        pltpu.make_async_remote_copy(
            src_ref=msg.at[j, dest],
            dst_ref=got.at[j, z],
            send_sem=c_send.at[j],
            recv_sem=c_recv.at[j],
            device_id=(me, dest),
            device_id_type=MESH,
        ).start()

    for j in range(CHUNKS):
        cols = pl.ds(j * CW, CW)
        normed = (mixf[:, cols] * scale * gainb[:, cols]).astype(BF16)
        stacked = jnp.concatenate(
            [normed[:, k * HD : (k + 1) * HD] for k in range(KB)], axis=0
        )
        sent = nn(pick[...], stacked).reshape(NZ, CAP * KB, HD)
        msg[j] = sent.astype(BF16)
        c_copy(j, z_peer(8))

        @pl.loop(1, 8)
        def _(i):
            c_copy(j, z_peer(8 - i))
            c_copy(j, z_peer(8 + i))

        got[j, z] = msg[j, z]

    gathers = [
        Gather(
            lambda n, j=j: slots.at[j, n],
            lambda n, i, j=j: slots.at[j, n, :, pl.ds(i * (CW // 2), CW // 2)],
            lambda n, j=j: slots.at[j, pl.ds(0, n)],
            gs_sem.at[j], z, core, a, b,
        )
        for j in range(CHUNKS)
    ]

    def assemble(j):
        wait_for(got.at[j, pl.ds(0, NZ - 1)], c_recv.at[j])
        rows = got[j].astype(F32).reshape(ROWS * KB, HD).astype(BF16)
        ordered = nn(perm[...], rows).astype(BF16)
        for k in range(KB):
            slots[j, me, :, pl.ds(k * HD, HD)] = ordered[k * ROWS : (k + 1) * ROWS]
        gathers[j].start()

    half_slots = SLOTS // 2

    def experts(j):
        gathers[j].arrived()
        left = full_w[:, pl.ds(j * CW, CW)]
        for i in range(2):
            right = slots[j, pl.ds(i * 16, 16)].reshape(half_slots, CW)
            cols = pl.ds(i * half_slots, half_slots)
            product = nt(left, right)
            if j > 0:
                product = product + acc[:, cols]
            if j < CHUNKS - 1:
                acc[:, cols] = product
            else:
                g, v = product[:HID_HERE], product[HID_HERE:]
                hidden_out[:, cols] = (g / (1.0 + jnp.exp(-g)) * v).astype(BF16)

    g0, g1, g2 = gathers
    assemble(0)
    g0.step1()
    assemble(1)
    g0.step2()
    g1.step1()
    g0.step3()
    g0.step4()
    assemble(2)
    g1.step2()
    g2.step1()
    g0.step5()
    g1.step3()
    g1.step4()
    loads[7].wait()
    loads[8].wait()
    experts(0)
    g2.step2()
    g1.step5()
    g2.step3()
    g2.step4()
    experts(1)
    g2.step5()
    experts(2)

    wait_for(e1, st_sem.at[4])
    wait_for(fx.at[pl.ds(0, SIDE - 1)], st_sem.at[5])
    wait_for(fy.at[pl.ds(0, SIDE - 1)], st_sem.at[6])
    wait_for(sto, st_sem.at[7])
    wait_for(sb, rs_send.at[0])
    weights.finish()
    for j in range(CHUNKS):
        wait_for(msg.at[j, pl.ds(0, NZ - 1)], c_send.at[j])
        gathers[j].finish()


def per_device(queries, keys, values, decay, out_w, residual, gain, ids, gate, up):
    hbm = pl.BlockSpec(memory_space=pl.ANY)
    vmem = pltpu.VMEM
    dma = pltpu.SemaphoreType.DMA
    mixed, hidden = pl.pallas_call(
        kernel,
        out_shape=(
            jax.ShapeDtypeStruct((TOK, WIDTH), BF16),
            jax.ShapeDtypeStruct((HID_HERE, SLOTS), BF16),
        ),
        in_specs=[pl.BlockSpec(memory_space=pltpu.SMEM)] + [hbm] * 9,
        out_specs=(pl.BlockSpec(memory_space=vmem), pl.BlockSpec(memory_space=vmem)),
        scratch_shapes=[
            vmem((SPAN, 2 * HD), BF16),
            vmem((SPAN, 2 * HD), BF16),
            vmem((SPAN, 2 * HD), BF16),
            vmem((SPAN, OWN_COLS), BF16),
            vmem((TOK, WIDTH), BF16),
            vmem((1, WIDTH), F32),
            vmem((TOK, 2), jnp.int32),
            vmem((2 * SIDE * SIDE, OWN_COLS, SPAN), BF16),
            vmem((2 * HID_HERE, WIDTH), BF16),
            vmem((2, HD, HD), F32),
            vmem((HD, HD), F32),
            vmem((SIDE, HD, HD), BF16),
            vmem((SIDE, HD, HD), BF16),
            vmem((2, HD, HD), F32),
            vmem((HD, HD), F32),
            vmem((2, SPAN, HD), F32),
            vmem((SPAN, 2 * HD), BF16),
            vmem((NZ, TOK, WIDTH), F32),
            vmem((NZ - 1, TOK, WIDTH), BF16),
            vmem((NZ - 1, TOK, WIDTH), BF16),
            vmem((TOK, WIDTH), F32),
            vmem((ROWS * KB, HD), BF16),
            vmem((ROWS * KB, ROWS * KB), BF16),
            vmem((CHUNKS, NZ, CAP * KB, HD), BF16),
            vmem((CHUNKS, NZ, CAP * KB, HD), BF16),
            vmem((CHUNKS, 2 * SIDE * SIDE, ROWS, CW), BF16),
            vmem((2 * HID_HERE, SLOTS), F32),
            dma((9,)),
            dma((8,)),
            dma((8,)),
            dma((CHUNKS, 8)),
            dma((NZ - 1, PIECES)),
            dma((1,)),
            dma((CHUNKS,)),
            dma((CHUNKS,)),
        ],
        compiler_params=pltpu.CompilerParams(
            collective_id=0, has_side_effects=True, vmem_limit_bytes=60000000
        ),
        name="block",
    )(
        decay, queries, keys, values, out_w, residual, gain.reshape(1, WIDTH), ids, gate, up
    )
    return mixed, hidden[None]


def solution(mesh):
    in_specs = (
        P("ctx", "exp"),
        P("ctx", "exp"),
        P("ctx", "exp"),
        P("exp"),
        P("exp", "ctx"),
        P(("ctx", "exp"), None),
        P(),
        P(("ctx", "exp"), None),
        P("exp", "ctx", None),
        P("exp", "ctx", None),
    )
    out_specs = (P(("ctx", "exp"), None), P("exp", "ctx", None))
    return jax.shard_map(
        per_device, mesh=mesh, in_specs=in_specs, out_specs=out_specs, check_vma=False
    )
```

time: 383 us -> 113 us (0.30)
  waiting for transfers between devices: 218 us -> 0 us
  Pallas kernels: 0 us -> 106 us
  blocking collectives: 89.9 us -> 0 us
  other arithmetic: 35.2 us -> 0 us
  matrix products: 19.3 us -> 0 us
  between operations: 14.7 us -> 0.65 us
    all_gather x4 -> x0, waiting for transfers between devices: 150 us -> none  [the longest x1 78.5 us: per_device(): piece = lax.all_gather(received, 'ctx', axis=0, tiled=True)]
    pallas_call x0 -> x1, Pallas kernels: none -> 106 us  [per_device(): pl.pallas_call(kernel, out_shape=(jax.ShapeDtypeStruct((TOK, WIDTH), BF16...]
    unnamed x1 -> x0, blocking collectives: 69 us -> none
    reduce_scatter x1 -> x0, waiting for transfers between devices: 67 us -> none  [per_device(): lax.psum_scatter(partial_rows, 'exp', scatter_dimension=0, tiled=True)]
    select_n x33 -> x0, other arithmetic: 31.9 us -> none  [the longest x32 31.9 us: hop(): return jax.tree.map(lambda a, b: jnp.where(reached, a, b), new, before)]
    all_gather x1 -> x0, blocking collectives: 20.9 us -> none  [per_device(): lax.all_gather(expert_ids.astype(jnp.bfloat16), 'exp', axis=0, tiled=True)]
    dot_general x8 -> x0, matrix products: 19.3 us -> none  [the longest x1 7.08 us: per_device(): lax.dot_general(gate_here, piece, contract, preferred_element_type=jnp.fl...]
    unnamed x20 -> x6, local copies, waits for them, and re-layouts: 1.32 us -> 6.22 us
  transfers between devices with their start and end apart: 5 -> 0, of which waited for: 4 -> 0; matrix products, arithmetic and copies ran while one was open for 9% -> 0% of each run, Pallas kernels for 0% -> 0%
where the time goes in v1:
time: 113 us
  Pallas kernels  106 us (94%)
  local copies, waits for them, and re-layouts  6.22 us (6%)
    pallas_call x1, Pallas kernels, per_device(): pl.pallas_call(kernel, out_shape=(jax.ShapeDtypeStruct((TOK, WIDTH), BF16...  106 us
    unnamed x6, local copies, waits for them, and re-layouts  6.22 us

profile of v1, /device:TPU:1, one launch (start us, length us, event | category | flops | bytes accessed | tf_op | source)
XLA Modules:
  0.0 112.9 jit_solution(2577341962790332420)
XLA Ops:
  0.6 0.0 copy-start
  0.6 0.7 copy-done
  1.3 0.7 copy.13.ids_hbm
  2.0 1.5 %copy.12.w_hbm = bf16[256,96]{1,0:T(8,128)(2,1)} copy(bf16[256,96]{0,1:T(8,128)(2,1)} %param.14) | data formatting | bytes 98304 | tf_op args[4]
  3.5 106.0 %block.1 = (bf16[16,3072]{1,0:T(8,128)(2,1)}, bf16[144,1536]{1,0:T(8,128)(2,1)}) custom-call(f32[2]{0:T(128)} %decay.1, bf16[256,256]{1,0:T(8,128)(2,1)} %q_hbm.1, bf16[256,256]{1,0:T(8,128)(2,1)} %k_hbm.1, bf16[256,256]{1,0:T(8,128)(2,1)} %v_hbm.1, bf16[256,96]{1,0:T(8,128)(2,1)} %copy.12.w_hbm, bf16[16,3072]{1,0:T(8,128)(2,1)} %res_hbm.1, ...), custom_call_target="tpu_custom_call" | custom-call | tf_op jit(solution)/shard_map/block/pallas_call | solution.py:481
  109.5 1.5 %copy.16 = bf16[16,3072]{1,0:T(8,128)(2,1)} copy(bf16[16,3072]{1,0:T(8,128)(2,1)} %get-tuple-element.8) | data formatting | bytes 196608
  111.1 1.8 %copy.17 = bf16[1,144,1536]{2,1,0:T(8,128)(2,1)} copy(bf16[1,144,1536]{2,1,0:T(8,128)(2,1)} %bitcast.2) | data formatting | bytes 884736
Async XLA Ops:
  0.6 0.7 copy-start

commit v2 on v1

--- a/solution.py
+++ b/solution.py
@@ -25,6 +25,7 @@
 PW = WIDTH // PIECES
 HID_HERE = 144
 SLOTS = 1536
+PART = SLOTS // SIDE
 
 A1, A2, B1A, B1B, B2A, B2B, XC, SENT = range(8)
 
@@ -131,12 +132,67 @@
         self.wait(SENT, 31)
 
 
+class Slots:
+    def __init__(self, blocks, sems, plane, b, a):
+        self.blocks, self.sems, self.plane, self.b, self.a = blocks, sems, plane, b, a
+        self.core = plane.core
+
+    def send(self, src, dst, sem, ctx):
+        pltpu.make_async_remote_copy(
+            src_ref=src,
+            dst_ref=dst,
+            send_sem=self.sems.at[4],
+            recv_sem=self.sems.at[sem],
+            device_id=(ctx, self.plane.z),
+            device_id_type=MESH,
+        ).start()
+
+    def wait(self, sem, count):
+        ref = self.blocks.at[pl.ds(0, count)]
+        pltpu.make_async_copy(ref, ref, self.sems.at[sem]).wait()
+
+    def along(self, core, sem):
+        ref = self.blocks.at[2 * self.b + core]
+        for e in (1, -1):
+            self.send(ref, ref, sem, self.plane.at(0, e))
+
+    def start(self):
+        own = self.blocks.at[2 * self.b + self.core]
+        partner = self.plane.at(0, 0) + 1 - 2 * self.core
+        self.send(own, self.blocks.at[2 * self.a + self.core], 0, partner)
+        self.along(self.core, 1)
+
+    def step1(self):
+        self.wait(0, 1)
+        self.along(1 - self.core, 2)
+
+    def relay(self, core):
+        for e in (1, -1):
+            chip = lax.rem(self.b + (SIDE - e), SIDE)
+            ref = self.blocks.at[2 * chip + core, :, pl.ds((1 - e) // 2 * (CW // 2), CW // 2)]
+            self.send(ref, ref, 3, self.plane.at(0, e))
+
+    def step2(self):
+        self.wait(1, 2)
+        self.relay(self.core)
+
+    def step3(self):
+        self.wait(2, 2)
+        self.relay(1 - self.core)
+
+    def arrived(self):
+        self.wait(3, 2)
+
+    def finish(self):
+        self.wait(4, 7)
+
+
 def kernel(
     decay, q_hbm, k_hbm, v_hbm, w_hbm, res_hbm, gain_hbm, ids_hbm, gate_hbm, up_hbm,
     mixed_out, hidden_out,
-    qb, kb, vb, wb, resb, gainb, idsb, wg, full_w, fr, e1, fx, fy, st, sto, att, ho,
-    part, sb, rb, mixf, pick, perm, msg, got, slots, acc,
-    load_sem, st_sem, gw_sem, gs_sem, rs_recv, rs_send, c_recv, c_send,
+    qb, kb, vb, resb, gainb, idsb, wg, full_w, fr, e1, fx, fy, st, sto, att, ho,
+    part, sb, rb, mixf, pick, perm, msg, got, slots, acc, ours, hid,
+    load_sem, st_sem, gw_sem, gs_sem, bulk_sem, hid_sem, rs_recv, rs_send, c_recv, c_send,
 ):
     me, z = lax.axis_index("ctx"), lax.axis_index("exp")
     core = lax.rem(me, 2)
@@ -164,18 +220,17 @@
         greet(x_peer(d), z)
         greet(y_peer(d), z)
 
-    @pl.loop(1, NZ)
-    def _(d):
-        greet(me, z_peer(d))
+    greet(me, z_peer(1))
+    greet(me, z_peer(NZ - 1))
 
     loads = [
         pltpu.make_async_copy(src, dst, load_sem.at[i])
         for i, (src, dst) in enumerate(
             (
-                (k_hbm, kb), (v_hbm, vb), (w_hbm, wb), (q_hbm, qb), (ids_hbm, idsb),
+                (k_hbm, kb), (v_hbm, vb), (w_hbm, wg.at[me]), (q_hbm, qb), (ids_hbm, idsb),
                 (res_hbm, resb), (gain_hbm, gainb),
-                (gate_hbm.at[0], full_w.at[pl.ds(0, HID_HERE)]),
-                (up_hbm.at[0], full_w.at[pl.ds(HID_HERE, HID_HERE)]),
+                (gate_hbm.at[0], full_w.at[a, pl.ds(0, HID_HERE)]),
+                (up_hbm.at[0], full_w.at[a, pl.ds(HID_HERE, HID_HERE)]),
             )
         )
     ]
@@ -194,10 +249,6 @@
         value = vb[:, cols]
         fr[h] = nn(hi, value) + nn(lo, value)
 
-    loads[2].wait()
-    small = one_hot(iota((OWN_COLS, OWN_COLS), 0) == iota((OWN_COLS, OWN_COLS), 1))
-    wg[me] = nt(small, wb[...]).astype(BF16)
-
     weights = Gather(
         lambda n: wg.at[n],
         lambda n, i: wg.at[n, :, pl.ds(i * HD, HD)],
@@ -205,7 +256,8 @@
         gw_sem, z, core, a, b,
     )
 
-    pl.semaphore_wait(barrier, 1 + 2 * (SIDE - 1) + NZ - 1)
+    pl.semaphore_wait(barrier, 1 + 2 * (SIDE - 1) + 2)
+    loads[2].wait()
 
     def state_send(src, dst, i, ctx):
         pltpu.make_async_remote_copy(
@@ -281,18 +333,16 @@
     weights.step4()
 
     loads[4].wait()
-    lane = iota((TOK, HD), 1)
-    expert = lax.shift_right_logical(lane * 43, 7)
-    ids = idsb[...]
-    named = one_hot((ids[:, 0:1] == expert) | (ids[:, 1:2] == expert))
-    lower = one_hot(iota((TOK, TOK), 0) > iota((TOK, TOK), 1))
-    rank = nn(lower, named)
-    place = (lane - CAP * expert).astype(F32)
-    chosen = jnp.where(rank == place, named.astype(F32), 0.0).astype(BF16)
-    turned = nt(eye, chosen).astype(BF16)
+    line = iota((HD, TOK), 0)
+    expert = lax.shift_right_logical(line * 43, 7)
+    named = one_hot((idsb[0:1, :] == expert) | (idsb[1:2, :] == expert))
+    upper = one_hot(iota((TOK, TOK), 0) < iota((TOK, TOK), 1))
+    rank = nn(named, upper)
+    place = (line - CAP * expert).astype(F32)
+    turned = jnp.where(rank == place, named.astype(F32), 0.0).astype(BF16)
     tall = (ROWS * KB, HD)
     spread = one_hot(lax.shift_right_logical(iota(tall, 0), 3) == iota(tall, 1))
-    again = one_hot(jnp.bitwise_and(lane, TOK - 1) == iota((TOK, HD), 0))
+    again = one_hot(jnp.bitwise_and(iota((TOK, HD), 1), TOK - 1) == iota((TOK, HD), 0))
     table = nn(nn(spread, turned).astype(BF16), again)
     here = jnp.bitwise_and(iota(tall, 0), KB - 1) == lax.shift_right_logical(iota(tall, 1), 4)
     pick[...] = jnp.where(here, table, 0.0).astype(BF16)
@@ -310,6 +360,21 @@
         attended = att[h] + (nn(query, hi) + nn(query, lo)) * inner
         mean = jnp.mean(attended * attended, axis=-1, keepdims=True)
         ho[:, cols] = (attended * lax.rsqrt(mean + 1e-05)).astype(BF16)
+
+    def bulk_send(ref, sem, da):
+        pltpu.make_async_remote_copy(
+            src_ref=ref,
+            dst_ref=ref,
+            send_sem=bulk_sem.at[2],
+            recv_sem=bulk_sem.at[sem],
+            device_id=(weights.at(da, 0), z),
+            device_id_type=MESH,
+        ).start()
+
+    loads[7].wait()
+    loads[8].wait()
+    for d in (1, -1):
+        bulk_send(full_w.at[a], 0, d)
 
     weights.arrived()
 
@@ -358,6 +423,12 @@
 
     for n in range(PIECES):
         rs_step(7, n, sign(n), z_peer(NZ + sign(n)))
+
+    wait_for(full_w.at[pl.ds(0, 2)], bulk_sem.at[0])
+    for d in (1, -1):
+        chip = lax.rem(a + (SIDE - d), SIDE)
+        half = pl.ds((1 - d) // 2 * (WIDTH // 2), WIDTH // 2)
+        bulk_send(full_w.at[chip, :, half], 1, d)
 
     loads[5].wait()
     loads[6].wait()
@@ -403,65 +474,78 @@
 
         got[j, z] = msg[j, z]
 
-    gathers = [
-        Gather(
-            lambda n, j=j: slots.at[j, n],
-            lambda n, i, j=j: slots.at[j, n, :, pl.ds(i * (CW // 2), CW // 2)],
-            lambda n, j=j: slots.at[j, pl.ds(0, n)],
-            gs_sem.at[j], z, core, a, b,
-        )
-        for j in range(CHUNKS)
-    ]
+    gathers = [Slots(slots.at[j], gs_sem.at[j], weights, b, a) for j in range(CHUNKS)]
 
     def assemble(j):
         wait_for(got.at[j, pl.ds(0, NZ - 1)], c_recv.at[j])
         rows = got[j].astype(F32).reshape(ROWS * KB, HD).astype(BF16)
         ordered = nn(perm[...], rows).astype(BF16)
         for k in range(KB):
-            slots[j, me, :, pl.ds(k * HD, HD)] = ordered[k * ROWS : (k + 1) * ROWS]
+            slots[j, 2 * b + core, :, pl.ds(k * HD, HD)] = ordered[k * ROWS : (k + 1) * ROWS]
         gathers[j].start()
 
-    half_slots = SLOTS // 2
-
-    def experts(j):
-        gathers[j].arrived()
-        left = full_w[:, pl.ds(j * CW, CW)]
-        for i in range(2):
-            right = slots[j, pl.ds(i * 16, 16)].reshape(half_slots, CW)
-            cols = pl.ds(i * half_slots, half_slots)
-            product = nt(left, right)
-            if j > 0:
-                product = product + acc[:, cols]
-            if j < CHUNKS - 1:
-                acc[:, cols] = product
+    def product(j, i):
+        right = slots[j].reshape(PART, CW)
+        return nt(full_w[i, :, pl.ds(j * CW, CW)], right)
+
+    def experts(j, parts):
+        for i in parts:
+            if j == 0:
+                acc[i] = product(j, i)
             else:
-                g, v = product[:HID_HERE], product[HID_HERE:]
-                hidden_out[:, cols] = (g / (1.0 + jnp.exp(-g)) * v).astype(BF16)
+                acc[i] = acc[i] + product(j, i)
 
     g0, g1, g2 = gathers
     assemble(0)
     g0.step1()
+    g0.step2()
+    g0.step3()
     assemble(1)
-    g0.step2()
     g1.step1()
-    g0.step3()
-    g0.step4()
+    g1.step2()
+    g1.step3()
+    g0.arrived()
+    wait_for(full_w.at[0], bulk_sem.at[1])
+    experts(0, (0, 1))
     assemble(2)
-    g1.step2()
     g2.step1()
-    g0.step5()
-    g1.step3()
-    g1.step4()
-    loads[7].wait()
-    loads[8].wait()
-    experts(0)
+    experts(0, (2,))
     g2.step2()
-    g1.step5()
+    experts(0, (3,))
     g2.step3()
-    g2.step4()
-    experts(1)
-    g2.step5()
-    experts(2)
+    g1.arrived()
+    experts(1, range(SIDE))
+    g2.arrived()
+    for d in (2, 1, 3, 0):
+        i = lax.rem(a + d, SIDE)
+        total = acc[i] + product(CHUNKS - 1, i)
+        g, v = total[:HID_HERE], total[HID_HERE:]
+        value = (g / (1.0 + jnp.exp(-g)) * v).astype(BF16)
+        if d == 0:
+            hid[a] = value
+        else:
+            ours[i] = value
+            pltpu.make_async_remote_copy(
+                src_ref=ours.at[i],
+                dst_ref=hid.at[a],
+                send_sem=hid_sem.at[1],
+                recv_sem=hid_sem.at[0],
+                device_id=(weights.at(d, 0), z),
+                device_id_type=MESH,
+            ).start()
+    wait_for(hid.at[pl.ds(0, SIDE - 1)], hid_sem.at[0])
+
+    @pl.when(core == 1)
+    def _():
+        for i in range(SIDE):
+            hidden_out[:, pl.ds(i * PART, PART)] = hid[i]
+
+    @pl.when(core == 0)
+    def _():
+        step = 2 * ROWS
+        for i in range(SIDE):
+            pieces = [hid[k].astype(F32)[:, i * step : (i + 1) * step] for k in range(SIDE)]
+            hidden_out[:, pl.ds(i * PART, PART)] = jnp.concatenate(pieces, axis=1).astype(BF16)
 
     wait_for(e1, st_sem.at[4])
     wait_for(fx.at[pl.ds(0, SIDE - 1)], st_sem.at[5])
@@ -469,6 +553,8 @@
     wait_for(sto, st_sem.at[7])
     wait_for(sb, rs_send.at[0])
     weights.finish()
+    wait_for(full_w.at[pl.ds(0, SIDE - 1)], bulk_sem.at[2])
+    wait_for(ours.at[pl.ds(0, SIDE - 1)], hid_sem.at[1])
     for j in range(CHUNKS):
         wait_for(msg.at[j, pl.ds(0, NZ - 1)], c_send.at[j])
         gathers[j].finish()
@@ -490,12 +576,11 @@
             vmem((SPAN, 2 * HD), BF16),
             vmem((SPAN, 2 * HD), BF16),
             vmem((SPAN, 2 * HD), BF16),
-            vmem((SPAN, OWN_COLS), BF16),
             vmem((TOK, WIDTH), BF16),
             vmem((1, WIDTH), F32),
-            vmem((TOK, 2), jnp.int32),
+            vmem((2, TOK), jnp.int32),
             vmem((2 * SIDE * SIDE, OWN_COLS, SPAN), BF16),
-            vmem((2 * HID_HERE, WIDTH), BF16),
+            vmem((SIDE, 2 * HID_HERE, WIDTH), BF16),
             vmem((2, HD, HD), F32),
             vmem((HD, HD), F32),
             vmem((SIDE, HD, HD), BF16),
@@ -512,12 +597,16 @@
             vmem((ROWS * KB, ROWS * KB), BF16),
             vmem((CHUNKS, NZ, CAP * KB, HD), BF16),
             vmem((CHUNKS, NZ, CAP * KB, HD), BF16),
-            vmem((CHUNKS, 2 * SIDE * SIDE, ROWS, CW), BF16),
-            vmem((2 * HID_HERE, SLOTS), F32),
+            vmem((CHUNKS, 2 * SIDE, ROWS, CW), BF16),
+            vmem((SIDE, 2 * HID_HERE, PART), F32),
+            vmem((SIDE, HID_HERE, PART), BF16),
+            vmem((SIDE, HID_HERE, PART), BF16),
             dma((9,)),
             dma((8,)),
             dma((8,)),
-            dma((CHUNKS, 8)),
+            dma((CHUNKS, 5)),
+            dma((3,)),
+            dma((2,)),
             dma((NZ - 1, PIECES)),
             dma((1,)),
             dma((CHUNKS,)),
@@ -528,7 +617,7 @@
         ),
         name="block",
     )(
-        decay, queries, keys, values, out_w, residual, gain.reshape(1, WIDTH), ids, gate, up
+        decay, queries, keys, values, out_w.T, residual, gain.reshape(1, WIDTH), ids.T, gate, up
     )
     return mixed, hidden[None]
 

time: 113 us -> 98.7 us (0.87)
  Pallas kernels: 106 us -> 93.8 us
  local copies, waits for them, and re-layouts: 6.22 us -> 3.34 us
    pallas_call x1, Pallas kernels: 106 us -> 93.8 us  [per_device(): pl.pallas_call(kernel, out_shape=(jax.ShapeDtypeStruct((TOK, WIDTH), BF16...]
    unnamed x6 -> x2, local copies, waits for them, and re-layouts: 6.22 us -> 3.34 us
where the time goes in v2:
time: 98.7 us; the launch traced here: 97.8 us
  Pallas kernels  93.8 us (95%)
  local copies, waits for them, and re-layouts  3.34 us (3%)
    pallas_call x1, Pallas kernels, per_device(): pl.pallas_call(kernel, out_shape=(jax.ShapeDtypeStruct((TOK, WIDTH), BF16...  93.8 us
    unnamed x2, local copies, waits for them, and re-layouts  3.34 us

profile of v2, /device:TPU:1, one launch (start us, length us, event | category | flops | bytes accessed | tf_op | source)
XLA Modules:
  0.0 97.8 jit_solution(16491682090665688453)
XLA Ops:
  0.6 93.8 %block.1 = (bf16[16,3072]{1,0:T(8,128)(2,1)}, bf16[144,1536]{1,0:T(8,128)(2,1)}) custom-call(f32[2]{0:T(128)} %decay.1, bf16[256,256]{1,0:T(8,128)(2,1)} %q_hbm.1, bf16[256,256]{1,0:T(8,128)(2,1)} %k_hbm.1, bf16[256,256]{1,0:T(8,128)(2,1)} %v_hbm.1, bf16[96,256]{1,0:T(8,128)(2,1)} %bitcast.5, bf16[16,3072]{1,0:T(8,128)(2,1)} %res_hbm.1, f32[1,3072]{1,0:T(1,128)} %bitcast.6, ...), custom_call_target="tpu_custom_call" | custom-call | tf_op jit(solution)/shard_map/block/pallas_call | solution.py:567
  94.5 1.5 %copy.14 = bf16[16,3072]{1,0:T(8,128)(2,1)} copy(bf16[16,3072]{1,0:T(8,128)(2,1)} %get-tuple-element.8) | data formatting | bytes 196608
  96.0 1.8 %copy.15 = bf16[1,144,1536]{2,1,0:T(8,128)(2,1)} copy(bf16[1,144,1536]{2,1,0:T(8,128)(2,1)} %bitcast.4) | data formatting | bytes 884736

commit v3 on v2

--- a/solution.py
+++ b/solution.py
@@ -122,6 +122,8 @@
         self.wait(B2A, 3)
         for da in (0, 1, -1):
             self.across(self.at(da, 2))
+
+    def step6(self):
         self.wait(B2B, 1)
         self.across(self.at(2, 2))
 
@@ -151,20 +153,15 @@
         ref = self.blocks.at[pl.ds(0, count)]
         pltpu.make_async_copy(ref, ref, self.sems.at[sem]).wait()
 
-    def along(self, core, sem):
-        ref = self.blocks.at[2 * self.b + core]
-        for e in (1, -1):
-            self.send(ref, ref, sem, self.plane.at(0, e))
-
     def start(self):
         own = self.blocks.at[2 * self.b + self.core]
-        partner = self.plane.at(0, 0) + 1 - 2 * self.core
-        self.send(own, self.blocks.at[2 * self.a + self.core], 0, partner)
-        self.along(self.core, 1)
-
-    def step1(self):
-        self.wait(0, 1)
-        self.along(1 - self.core, 2)
+        there = self.blocks.at[2 * self.a + self.core]
+        turn = 1 - 2 * self.core
+        for e in (1, -1):
+            self.send(own, own, 1, self.plane.at(0, e))
+        for e in (1, -1):
+            self.send(own, there, 2, self.plane.at(e, 0) + turn)
+        self.send(own, there, 0, self.plane.at(0, 0) + turn)
 
     def relay(self, core):
         for e in (1, -1):
@@ -181,6 +178,7 @@
         self.relay(1 - self.core)
 
     def arrived(self):
+        self.wait(0, 1)
         self.wait(3, 2)
 
     def finish(self):
@@ -191,7 +189,7 @@
     decay, q_hbm, k_hbm, v_hbm, w_hbm, res_hbm, gain_hbm, ids_hbm, gate_hbm, up_hbm,
     mixed_out, hidden_out,
     qb, kb, vb, resb, gainb, idsb, wg, full_w, fr, e1, fx, fy, st, sto, att, ho,
-    part, sb, rb, mixf, pick, perm, msg, got, slots, acc, ours, hid,
+    part, sb, rb, pick, perm, msg, got, slots, acc, ours, hid, mixf,
     load_sem, st_sem, gw_sem, gs_sem, bulk_sem, hid_sem, rs_recv, rs_send, c_recv, c_send,
 ):
     me, z = lax.axis_index("ctx"), lax.axis_index("exp")
@@ -320,6 +318,8 @@
     local_part(1)
     weights.step2()
     weights.step3()
+    weights.step4()
+    weights.step5()
 
     wait_for(fy.at[pl.ds(0, SIDE - 1)], st_sem.at[2])
     above = jnp.zeros((HD, HD), F32)
@@ -330,7 +330,7 @@
     st[core] = jnp.where(core == 0, state0, state1)
     sto[...] = jnp.where(core == 0, state1, state0)
     state_send(sto, st.at[core], 3, partner)
-    weights.step4()
+    weights.step6()
 
     loads[4].wait()
     line = iota((HD, TOK), 0)
@@ -351,7 +351,6 @@
     perm[...] = one_hot(iota(square, 1) == KB * (iota(square, 0) - ROWS * block) + block)
 
     wait_for(st.at[0], st_sem.at[3])
-    weights.step5()
     for h in range(2):
         cols = pl.ds(h * HD, HD)
         query = qb[:, cols]
@@ -379,7 +378,7 @@
     weights.arrived()
 
     def sign(n):
-        return 1 if n < PIECES // 2 else -1
+        return 1 - 2 * (n % 2)
 
     def rs_send_to(i, n, d):
         cols = pl.ds(n * PW, PW)
@@ -396,12 +395,11 @@
         wait_for(rb.at[i, :, pl.ds(n * PW, PW)], rs_recv.at[i, n])
 
     SHORT = NZ // 2
-    heads = ho[...]
-    flat = wg[...].reshape(WIDTH, SPAN)
-    for n in range(PIECES):
+
+    def rs_first(n):
         cols = pl.ds(n * PW, PW)
-        rows = nt(heads, flat[n * PW : (n + 1) * PW])
-        part[:, :, cols] = rows.reshape(NZ, TOK, PW)
+        columns = wg[...].reshape(WIDTH, SPAN)[n * PW : (n + 1) * PW]
+        part[:, :, cols] = nt(ho[...], columns).reshape(NZ, TOK, PW)
         sb[0, :, cols] = part[z_peer(8), :, cols].astype(BF16)
         rs_send_to(0, n, sign(n))
         sb[SHORT, :, cols] = part[z_peer(NZ - 7 * sign(n)), :, cols].astype(BF16)
@@ -414,26 +412,7 @@
         sb[i, :, cols] = value.astype(BF16)
         rs_send_to(i, n, d)
 
-    @pl.loop(1, 7)
-    def _(i):
-        for n in range(PIECES):
-            s = sign(n)
-            rs_step(i, n, s, z_peer(NZ + s * (8 - i)))
-            rs_step(SHORT + i, n, -s, z_peer(NZ - s * (7 - i)))
-
-    for n in range(PIECES):
-        rs_step(7, n, sign(n), z_peer(NZ + sign(n)))
-
-    wait_for(full_w.at[pl.ds(0, 2)], bulk_sem.at[0])
-    for d in (1, -1):
-        chip = lax.rem(a + (SIDE - d), SIDE)
-        half = pl.ds((1 - d) // 2 * (WIDTH // 2), WIDTH // 2)
-        bulk_send(full_w.at[chip, :, half], 1, d)
-
-    loads[5].wait()
-    loads[6].wait()
-    squares = jnp.zeros((TOK, HD), F32)
-    for n in range(PIECES):
+    def rs_last(n):
         cols = pl.ds(n * PW, PW)
         wait_piece(SHORT + 6, n)
         wait_piece(7, n)
@@ -442,22 +421,30 @@
         mixed_out[:, cols] = rounded
         rounded = rounded.astype(F32)
         mixf[:, cols] = rounded
-        power2 = rounded * rounded
-        for i in range(PW // HD):
-            squares = squares + power2[:, i * HD : (i + 1) * HD]
-    scale = lax.rsqrt(jnp.sum(squares, axis=-1, keepdims=True) / WIDTH + 1e-05)
-
-    def c_copy(j, dest):
+        squared = rounded * rounded
+        return sum(squared[:, i * HD : (i + 1) * HD] for i in range(PW // HD))
+
+    def c_copy(src, dst, sems, dest):
         pltpu.make_async_remote_copy(
-            src_ref=msg.at[j, dest],
-            dst_ref=got.at[j, z],
-            send_sem=c_send.at[j],
-            recv_sem=c_recv.at[j],
+            src_ref=src,
+            dst_ref=dst,
+            send_sem=sems[0],
+            recv_sem=sems[1],
             device_id=(me, dest),
             device_id_type=MESH,
         ).start()
 
-    for j in range(CHUNKS):
+    def to_all(src, dst, sems):
+        c_copy(src.at[z_peer(8)], dst.at[z], sems, z_peer(8))
+
+        @pl.loop(1, 8)
+        def _(i):
+            c_copy(src.at[z_peer(8 - i)], dst.at[z], sems, z_peer(8 - i))
+            c_copy(src.at[z_peer(8 + i)], dst.at[z], sems, z_peer(8 + i))
+
+        dst[z] = src[z]
+
+    def dispatch(j, scale):
         cols = pl.ds(j * CW, CW)
         normed = (mixf[:, cols] * scale * gainb[:, cols]).astype(BF16)
         stacked = jnp.concatenate(
@@ -465,14 +452,31 @@
         )
         sent = nn(pick[...], stacked).reshape(NZ, CAP * KB, HD)
         msg[j] = sent.astype(BF16)
-        c_copy(j, z_peer(8))
-
-        @pl.loop(1, 8)
-        def _(i):
-            c_copy(j, z_peer(8 - i))
-            c_copy(j, z_peer(8 + i))
-
-        got[j, z] = msg[j, z]
+        to_all(msg.at[j], got.at[j], (c_send.at[j], c_recv.at[j]))
+
+    loads[5].wait()
+    loads[6].wait()
+    squares = jnp.zeros((TOK, HD), F32)
+    for i in range(9):
+        if i == 8:
+            wait_for(full_w.at[pl.ds(0, 2)], bulk_sem.at[0])
+            for d in (1, -1):
+                chip = lax.rem(a + (SIDE - d), SIDE)
+                half = pl.ds((1 - d) // 2 * (WIDTH // 2), WIDTH // 2)
+                bulk_send(full_w.at[chip, :, half], 1, d)
+        for n in range(PIECES):
+            s = sign(n)
+            if i == 0:
+                rs_first(n)
+            if 1 <= i <= 7:
+                rs_step(i, n, s, z_peer(NZ + s * (8 - i)))
+            if 1 <= i <= 6:
+                rs_step(SHORT + i, n, -s, z_peer(NZ - s * (7 - i)))
+            if i == 8:
+                squares = squares + rs_last(n)
+    scale = lax.rsqrt(jnp.sum(squares, axis=-1, keepdims=True) / WIDTH + 1e-05)
+    for j in range(CHUNKS):
+        dispatch(j, scale)
 
     gathers = [Slots(slots.at[j], gs_sem.at[j], weights, b, a) for j in range(CHUNKS)]
 
@@ -485,37 +489,25 @@
         gathers[j].start()
 
     def product(j, i):
-        right = slots[j].reshape(PART, CW)
-        return nt(full_w[i, :, pl.ds(j * CW, CW)], right)
-
-    def experts(j, parts):
-        for i in parts:
+        return nt(full_w[i, :, pl.ds(j * CW, CW)], slots[j].reshape(PART, CW))
+
+    def experts(j):
+        for i in range(SIDE):
             if j == 0:
                 acc[i] = product(j, i)
             else:
                 acc[i] = acc[i] + product(j, i)
 
-    g0, g1, g2 = gathers
-    assemble(0)
-    g0.step1()
-    g0.step2()
-    g0.step3()
-    assemble(1)
-    g1.step1()
-    g1.step2()
-    g1.step3()
-    g0.arrived()
+    for j in range(CHUNKS):
+        assemble(j)
+    for g in gathers:
+        g.step2()
+        g.step3()
     wait_for(full_w.at[0], bulk_sem.at[1])
-    experts(0, (0, 1))
-    assemble(2)
-    g2.step1()
-    experts(0, (2,))
-    g2.step2()
-    experts(0, (3,))
-    g2.step3()
-    g1.arrived()
-    experts(1, range(SIDE))
-    g2.arrived()
+    for j in range(CHUNKS):
+        gathers[j].arrived()
+        if j < CHUNKS - 1:
+            experts(j)
     for d in (2, 1, 3, 0):
         i = lax.rem(a + d, SIDE)
         total = acc[i] + product(CHUNKS - 1, i)
@@ -560,16 +552,33 @@
         gathers[j].finish()
 
 
+def emit(mixed, hidden, mixed_out, hidden_out, mixed_here, hidden_here, sem):
+    pairs = [(mixed, mixed_here, mixed_out)]
+    for i in range(3):
+        rows = pl.ds(i * 48, 48)
+        pairs.append((hidden.at[rows], hidden_here.at[rows], hidden_out.at[rows]))
+    into = [pltpu.make_async_copy(p[0], p[1], sem.at[0, i]) for i, p in enumerate(pairs)]
+    out = [pltpu.make_async_copy(p[1], p[2], sem.at[1, i]) for i, p in enumerate(pairs)]
+    for copy in into:
+        copy.start()
+    for first, second in zip(into, out):
+        first.wait()
+        second.start()
+    for copy in out:
+        copy.wait()
+
+
 def per_device(queries, keys, values, decay, out_w, residual, gain, ids, gate, up):
     hbm = pl.BlockSpec(memory_space=pl.ANY)
     vmem = pltpu.VMEM
     dma = pltpu.SemaphoreType.DMA
-    mixed, hidden = pl.pallas_call(
+    shapes = (
+        jax.ShapeDtypeStruct((TOK, WIDTH), BF16),
+        jax.ShapeDtypeStruct((HID_HERE, SLOTS), BF16),
+    )
+    results = pl.pallas_call(
         kernel,
-        out_shape=(
-            jax.ShapeDtypeStruct((TOK, WIDTH), BF16),
-            jax.ShapeDtypeStruct((HID_HERE, SLOTS), BF16),
-        ),
+        out_shape=shapes,
         in_specs=[pl.BlockSpec(memory_space=pltpu.SMEM)] + [hbm] * 9,
         out_specs=(pl.BlockSpec(memory_space=vmem), pl.BlockSpec(memory_space=vmem)),
         scratch_shapes=[
@@ -592,7 +601,6 @@
             vmem((NZ, TOK, WIDTH), F32),
             vmem((NZ - 1, TOK, WIDTH), BF16),
             vmem((NZ - 1, TOK, WIDTH), BF16),
-            vmem((TOK, WIDTH), F32),
             vmem((ROWS * KB, HD), BF16),
             vmem((ROWS * KB, ROWS * KB), BF16),
             vmem((CHUNKS, NZ, CAP * KB, HD), BF16),
@@ -601,6 +609,7 @@
             vmem((SIDE, 2 * HID_HERE, PART), F32),
             vmem((SIDE, HID_HERE, PART), BF16),
             vmem((SIDE, HID_HERE, PART), BF16),
+            vmem((TOK, WIDTH), F32),
             dma((9,)),
             dma((8,)),
             dma((8,)),
@@ -619,6 +628,15 @@
     )(
         decay, queries, keys, values, out_w.T, residual, gain.reshape(1, WIDTH), ids.T, gate, up
     )
+    mixed, hidden = pl.pallas_call(
+        emit,
+        out_shape=shapes,
+        in_specs=[hbm] * 2,
+        out_specs=(hbm, hbm),
+        scratch_shapes=[vmem((TOK, WIDTH), BF16), vmem((HID_HERE, SLOTS), BF16), dma((2, 4))],
+        compiler_params=pltpu.CompilerParams(vmem_limit_bytes=60000000),
+        name="emit",
+    )(*results)
     return mixed, hidden[None]
 
 

time: 98.7 us -> 88.5 us (0.90)
  Pallas kernels: 93.8 us -> 87.7 us
  local copies, waits for them, and re-layouts: 3.34 us -> 0 us
    pallas_call x1 -> x2, Pallas kernels: 93.8 us -> 87.7 us  [the longest x1 85.9 us: per_device(): pl.pallas_call(kernel, out_shape=shapes, in_specs=[pl.BlockSpec(memory_sp...]
    unnamed x2 -> x0, local copies, waits for them, and re-layouts: 3.34 us -> none
where the time goes in v3:
time: 88.5 us; the launch traced here: 88.3 us
  Pallas kernels  87.7 us (99%)
    pallas_call x1, Pallas kernels, per_device(): pl.pallas_call(kernel, out_shape=shapes, in_specs=[pl.BlockSpec(memory_sp...  85.9 us
    pallas_call x1, Pallas kernels, per_device(): pl.pallas_call(emit, out_shape=shapes, in_specs=[hbm] * 2, out_specs=(hbm...  1.83 us

profile of v3, /device:TPU:1, one launch (start us, length us, event | category | flops | bytes accessed | tf_op | source)
XLA Modules:
  0.0 88.3 jit_solution(11707797101740414561)
XLA Ops:
  0.6 85.9 %block.1 = (bf16[16,3072]{1,0:T(8,128)(2,1)}, bf16[144,1536]{1,0:T(8,128)(2,1)}) custom-call(f32[2]{0:T(128)} %decay.1, bf16[256,256]{1,0:T(8,128)(2,1)} %q_hbm.1, bf16[256,256]{1,0:T(8,128)(2,1)} %k_hbm.1, bf16[256,256]{1,0:T(8,128)(2,1)} %v_hbm.1, bf16[96,256]{1,0:T(8,128)(2,1)} %bitcast.4, bf16[16,3072]{1,0:T(8,128)(2,1)} %res_hbm.1, f32[1,3072]{1,0:T(1,128)} %bitcast.5, ...), custom_call_target="tpu_custom_call" | custom-call | tf_op jit(solution)/shard_map/block/pallas_call | solution.py:579
  86.5 1.8 %emit.1 = (bf16[16,3072]{1,0:T(8,128)(2,1)}, bf16[144,1536]{1,0:T(8,128)(2,1)}) custom-call(bf16[16,3072]{1,0:T(8,128)(2,1)} %get-tuple-element.6.mixed, bf16[144,1536]{1,0:T(8,128)(2,1)} %get-tuple-element.7.hidden), custom_call_target="tpu_custom_call" | custom-call | tf_op jit(solution)/shard_map/emit/pallas_call | solution.py:631

commit v4 on v3

--- a/solution.py
+++ b/solution.py
@@ -332,24 +332,6 @@
     state_send(sto, st.at[core], 3, partner)
     weights.step6()
 
-    loads[4].wait()
-    line = iota((HD, TOK), 0)
-    expert = lax.shift_right_logical(line * 43, 7)
-    named = one_hot((idsb[0:1, :] == expert) | (idsb[1:2, :] == expert))
-    upper = one_hot(iota((TOK, TOK), 0) < iota((TOK, TOK), 1))
-    rank = nn(named, upper)
-    place = (line - CAP * expert).astype(F32)
-    turned = jnp.where(rank == place, named.astype(F32), 0.0).astype(BF16)
-    tall = (ROWS * KB, HD)
-    spread = one_hot(lax.shift_right_logical(iota(tall, 0), 3) == iota(tall, 1))
-    again = one_hot(jnp.bitwise_and(iota((TOK, HD), 1), TOK - 1) == iota((TOK, HD), 0))
-    table = nn(nn(spread, turned).astype(BF16), again)
-    here = jnp.bitwise_and(iota(tall, 0), KB - 1) == lax.shift_right_logical(iota(tall, 1), 4)
-    pick[...] = jnp.where(here, table, 0.0).astype(BF16)
-    square = (ROWS * KB, ROWS * KB)
-    block = lax.shift_right_logical(iota(square, 0) * 1366, 16)
-    perm[...] = one_hot(iota(square, 1) == KB * (iota(square, 0) - ROWS * block) + block)
-
     wait_for(st.at[0], st_sem.at[3])
     for h in range(2):
         cols = pl.ds(h * HD, HD)
@@ -453,6 +435,25 @@
         sent = nn(pick[...], stacked).reshape(NZ, CAP * KB, HD)
         msg[j] = sent.astype(BF16)
         to_all(msg.at[j], got.at[j], (c_send.at[j], c_recv.at[j]))
+
+    def tables():
+        loads[4].wait()
+        line = iota((HD, TOK), 0)
+        expert = lax.shift_right_logical(line * 43, 7)
+        named = one_hot((idsb[0:1, :] == expert) | (idsb[1:2, :] == expert))
+        upper = one_hot(iota((TOK, TOK), 0) < iota((TOK, TOK), 1))
+        rank = nn(named, upper)
+        place = (line - CAP * expert).astype(F32)
+        turned = jnp.where(rank == place, named.astype(F32), 0.0).astype(BF16)
+        tall = (ROWS * KB, HD)
+        spread = one_hot(lax.shift_right_logical(iota(tall, 0), 3) == iota(tall, 1))
+        again = one_hot(jnp.bitwise_and(iota((TOK, HD), 1), TOK - 1) == iota((TOK, HD), 0))
+        table = nn(nn(spread, turned).astype(BF16), again)
+        here = jnp.bitwise_and(iota(tall, 0), KB - 1) == lax.shift_right_logical(iota(tall, 1), 4)
+        pick[...] = jnp.where(here, table, 0.0).astype(BF16)
+        square = (ROWS * KB, ROWS * KB)
+        block = lax.shift_right_logical(iota(square, 0) * 1366, 16)
+        perm[...] = one_hot(iota(square, 1) == KB * (iota(square, 0) - ROWS * block) + block)
 
     loads[5].wait()
     loads[6].wait()
@@ -474,6 +475,8 @@
                 rs_step(SHORT + i, n, -s, z_peer(NZ - s * (7 - i)))
             if i == 8:
                 squares = squares + rs_last(n)
+        if i == 0:
+            tables()
     scale = lax.rsqrt(jnp.sum(squares, axis=-1, keepdims=True) / WIDTH + 1e-05)
     for j in range(CHUNKS):
         dispatch(j, scale)

time: 88.5 us -> 87.9 us (level)
  no operation moved by 1% of the time
where the time goes in v4:
time: 87.9 us; the launch traced here: 87.7 us
  Pallas kernels  87.1 us (99%)
    pallas_call x1, Pallas kernels, per_device(): pl.pallas_call(kernel, out_shape=shapes, in_specs=[pl.BlockSpec(memory_sp...  85.3 us
    pallas_call x1, Pallas kernels, per_device(): pl.pallas_call(emit, out_shape=shapes, in_specs=[hbm] * 2, out_specs=(hbm...  1.83 us

profile of v4, /device:TPU:1, one launch (start us, length us, event | category | flops | bytes accessed | tf_op | source)
XLA Modules:
  0.0 87.7 jit_solution(1020159024337623608)
XLA Ops:
  0.6 85.3 %block.1 = (bf16[16,3072]{1,0:T(8,128)(2,1)}, bf16[144,1536]{1,0:T(8,128)(2,1)}) custom-call(f32[2]{0:T(128)} %decay.1, bf16[256,256]{1,0:T(8,128)(2,1)} %q_hbm.1, bf16[256,256]{1,0:T(8,128)(2,1)} %k_hbm.1, bf16[256,256]{1,0:T(8,128)(2,1)} %v_hbm.1, bf16[96,256]{1,0:T(8,128)(2,1)} %bitcast.4, bf16[16,3072]{1,0:T(8,128)(2,1)} %res_hbm.1, f32[1,3072]{1,0:T(1,128)} %bitcast.5, ...), custom_call_target="tpu_custom_call" | custom-call | tf_op jit(solution)/shard_map/block/pallas_call | solution.py:582
  85.9 1.8 %emit.1 = (bf16[16,3072]{1,0:T(8,128)(2,1)}, bf16[144,1536]{1,0:T(8,128)(2,1)}) custom-call(bf16[16,3072]{1,0:T(8,128)(2,1)} %get-tuple-element.6.mixed, bf16[144,1536]{1,0:T(8,128)(2,1)} %get-tuple-element.7.hidden), custom_call_target="tpu_custom_call" | custom-call | tf_op jit(solution)/shard_map/emit/pallas_call | solution.py:634
